TPU v7x, 32 devices: a whole 2x2x4 slice. The times are simulated.
32 devices in a mesh: row: 4 (over x, core), col: 2 (over y), depth: 4 (over z).
Axes of the slice: x: 2, y: 2, z: 4, core: 2. Of those that a mesh axis runs over, the one named last changes fastest.
Arguments:
- tokens: bfloat16 [64, 6144], P(('col', 'depth'), 'row'), may hold values from -6 to 6
- first_weight: bfloat16 [6144, 24576], P('row', ('col', 'depth')), may hold values from -0.078125 to 0.078125
- first_tangent: bfloat16 [6144, 24576], P('row', ('col', 'depth')), may hold values from -0.078125 to 0.078125
- second_weight: bfloat16 [24576, 6144], P(('col', 'depth'), 'row'), may hold values from -0.0390625 to 0.0390625
- second_tangent: bfloat16 [24576, 6144], P(('col', 'depth'), 'row'), may hold values from -0.0390625 to 0.0390625
Outputs:
- grad_first: float32 [6144, 24576], P('row', ('col', 'depth'))
- grad_second: float32 [24576, 6144], P(('col', 'depth'), 'row')
All inputs are finite; a program needn't handle non-finite values.
Results may differ from a plain program's by a relative error of at most 0.0047.
Values may be sent and summed in bfloat16 or wider, within the bound.
A program may use at most 192 MiB of HBM per device.

v0:
```python
import math
import jax
import jax.numpy as jnp
from jax import lax
from jax.sharding import PartitionSpec as P


def gelu_parts(hidden, hidden_tan):
    inner = 0.7978845608 * (hidden + 0.044715 * hidden * hidden * hidden)
    tval = jnp.tanh(inner)
    active = (0.5 * hidden * (1.0 + tval)).astype(jnp.bfloat16)
    slopes = 0.5 * (1.0 + tval) + 0.5 * hidden * (1.0 - tval * tval) * 0.7978845608 * (
        1.0 + 3.0 * 0.044715 * hidden * hidden
    )
    active_tan = (slopes * hidden_tan).astype(jnp.bfloat16)
    return (active, active_tan, slopes)


def on_device(tokens, first_weight, first_tangent, second_weight, second_tangent):
    gathered = lax.all_gather(tokens, ("col", "depth"), axis=0, tiled=True)
    hidden = jnp.dot(gathered, first_weight, preferred_element_type=jnp.float32)
    hidden_tan = jnp.dot(gathered, first_tangent, preferred_element_type=jnp.float32)
    hidden, hidden_tan = lax.psum((hidden, hidden_tan), "row")
    active, active_tan, slopes = gelu_parts(hidden, hidden_tan)
    partial_value = jnp.dot(
        active_tan, second_weight, preferred_element_type=jnp.float32
    ) + jnp.dot(active, second_tangent, preferred_element_type=jnp.float32)
    out_tan = lax.psum(partial_value, ("col", "depth")).astype(jnp.bfloat16)
    backward = lax.dot_general(
        out_tan, second_weight, (((1,), (1,)), ((), ())), preferred_element_type=jnp.float32
    )
    backward = lax.psum(backward, "row")
    back_hidden = (backward * slopes).astype(jnp.bfloat16)
    factor = 1.0 / math.sqrt(gathered.shape[0])
    grad_second = (
        lax.dot_general(
            active, out_tan, (((0,), (0,)), ((), ())), preferred_element_type=jnp.float32
        )
        * factor
    )
    grad_first = (
        lax.dot_general(
            gathered, back_hidden, (((0,), (0,)), ((), ())), preferred_element_type=jnp.float32
        )
        * factor
    )
    return (grad_first, grad_second)


def solution(mesh):
    return jax.shard_map(
        on_device,
        mesh=mesh,
        in_specs=(
            P(("col", "depth"), "row"),
            P("row", ("col", "depth")),
            P("row", ("col", "depth")),
            P(("col", "depth"), "row"),
            P(("col", "depth"), "row"),
        ),
        out_specs=(P("row", ("col", "depth")), P(("col", "depth"), "row")),
        check_vma=False,
    )
```

profile of v0, /device:TPU:0, one launch (start us, length us, event | category | flops | bytes accessed | tf_op | source)
XLA Modules:
  0.0 220.9 jit_solution(1123703977794834401)
XLA Ops:
  7.2 0.0 slice-start.3
  7.2 0.0 all-reduce.7.cloned.1.call-start
  7.2 33.1 %all_gather.3 = bf16[64,1536]{1,0:T(8,128)(2,1)S(1)} all-gather(bf16[8,1536]{1,0:T(8,128)(2,1)} %param.5), channel_id=1, replica_groups=mesh['row'=4,'col'=2,'depth'=4] {'col','depth'}, dimensions={0}, use_global_device_ids=true | all-gather | bytes 221184 | tf_op jit(solution)/shard_map/all_gather | solution.py:20
  40.3 0.0 slice-start.4
  40.3 0.0 slice-start.5
  40.3 6.5 %fusion.12 = f32[64,3072]{1,0:T(8,128)} fusion(bf16[64,1536]{1,0:T(8,128)(2,1)S(1)} %all_gather.3, bf16[1536,3072]{1,0:T(8,128)(2,1)} %param.7), kind=kOutput, calls=%fused_computation.18 | convolution fusion | flops 603979776 | bytes 10420224 | tf_op jit(solution)/shard_map/dot_general | solution.py:22
  46.8 0.0 slice-done.3
  46.8 0.0 slice-done.4
  46.8 0.0 slice-done.5
  46.8 2.6 %fusion.11 = f32[64,3072]{1,0:T(8,128)} fusion(bf16[64,1536]{1,0:T(8,128)(2,1)S(1)} %all_gather.3, bf16[1536,3072]{1,0:T(8,128)(2,1)S(1)} %bitcast.15), kind=kOutput, calls=%fused_computation.17 | convolution fusion | flops 603979776 | bytes 10420224 | tf_op jit(solution)/shard_map/dot_general | solution.py:21
  49.4 0.0 slice-start
  49.4 0.0 all-reduce.7.cloned.1.call-update
  49.5 0.0 all-reduce.5.cloned.1.call-start
  49.5 44.0 %all-reduce.7.cloned.1.call-done = (f32[64,3072]{1,0:T(8,128)}, f32[64,3072]{1,0:T(8,128)}) async-done(((f32[64,3072]{1,0:T(8,128)}, f32[64,3072]{1,0:T(8,128)}), (f32[64,3072]{1,0:T(8,128)}, f32[64,3072]{1,0:T(8,128)})) %all-reduce.7.cloned.1.call-update) | async-done | bytes 1572880 | tf_op jit(solution)/shard_map/psum | solution.py:23
  93.5 0.0 slice-start.1
  93.5 0.0 slice-start.2
  93.5 0.0 copy-start
  93.5 6.3 %fusion.5 = f32[64,1536]{1,0:T(8,128)S(1)} fusion(bf16[3072,1536]{1,0:T(8,128)(2,1)} %param.8, f32[64,3072]{1,0:T(8,128)} %get-tuple-element.4, f32[64,3072]{1,0:T(8,128)} %get-tuple-element.5), kind=kOutput, calls=%fused_computation.13 | convolution fusion | flops 607715328 | bytes 11403264 | tf_op jit(solution)/shard_map/dot_general | solution.py:25
  99.8 0.0 slice-done
  99.8 0.0 slice-done.1
  99.8 0.3 slice-done.2
  100.1 0.1 copy-done
  100.2 1.8 convolution_add_fusion
  102.0 44.5 %all-reduce.8 = bf16[64,1536]{1,0:T(8,128)(2,1)S(1)} all-reduce(f32[64,1536]{1,0:T(8,128)S(1)} %convolution_add_fusion), channel_id=1, replica_groups=mesh['row'=4,'col'=2,'depth'=4] {'col','depth'}, use_global_device_ids=true, to_apply=%region_2.0 | all-reduce | flops 98304 | bytes 589824 | tf_op jit(solution)/shard_map/psum | solution.py:28
  146.5 7.5 %fusion.13 = f32[64,3072]{1,0:T(8,128)} fusion(bf16[64,1536]{1,0:T(8,128)(2,1)S(1)} %all-reduce.8, bf16[3072,1536]{1,0:T(8,128)(2,1)} %param.8), kind=kOutput, calls=%fused_computation.19 | convolution fusion | flops 603979776 | bytes 10420224 | tf_op jit(solution)/shard_map/dot_general | solution.py:29
  154.0 0.0 all-reduce.5.cloned.1.call-update
  154.0 8.3 %convolution_multiply_fusion = f32[3072,1536]{1,0:T(8,128)} fusion(bf16[64,1536]{1,0:T(8,128)(2,1)S(1)} %all-reduce.8, f32[64,3072]{1,0:T(8,128)S(1)} %copy-done), kind=kOutput, calls=%fused_computation.1 | convolution fusion | flops 610467840 | bytes 19857408 | tf_op jit(solution)/shard_map/dot_general | solution.py:36
  162.3 23.6 %all-reduce.5.cloned.1.call-done = f32[64,3072]{1,0:T(8,128)} async-done(((f32[64,3072]{1,0:T(8,128)}), f32[64,3072]{1,0:T(8,128)}) %all-reduce.5.cloned.1.call-update) | async-done | bytes 786448 | tf_op jit(solution)/shard_map/psum | solution.py:32
  185.9 9.6 %multiply_bitcast_fusion = f32[1536,3072]{0,1:T(8,128)} fusion(bf16[64,1536]{1,0:T(8,128)(2,1)S(1)} %all_gather.3, f32[64,3072]{1,0:T(8,128)} %all-reduce.5.cloned.1.call-done, f32[64,3072]{1,0:T(8,128)S(1)} %copy-done), kind=kOutput, calls=%fused_computation | convolution fusion | flops 612433920 | bytes 20643840 | tf_op jit(solution)/shard_map/dot_general | solution.py:42
  195.4 18.6 %copy.7 = f32[1536,3072]{1,0:T(8,128)} copy(f32[1536,3072]{0,1:T(8,128)} %multiply_bitcast_fusion) | data formatting | bytes 37748736
  (2 shorter events, 0.0 us)
Async XLA Ops:
  7.2 39.6 %slice-start.3 = ((s8[9437184]{0:T(1024)(128)(4,1)}), s8[1048576]{0:T(1024)(128)(4,1)S(1)}, s32[]{:S(2)}) async-start(s8[9437184]{0:T(1024)(128)(4,1)} %bitcast.14), calls=%async_computation.5 | async-start | bytes 2097152
  7.2 86.3 %all-reduce.7.cloned.1.call-start = ((), (), s32[]{:S(2)}) async-start(), calls=%async_computation.1 | async-start | bytes 3145728 | tf_op jit(solution)/shard_map/psum | solution.py:23
  40.3 6.5 %slice-start.4 = ((s8[9437184]{0:T(1024)(128)(4,1)}), s8[4194304]{0:T(1024)(128)(4,1)S(1)}, s32[]{:S(2)}) async-start(s8[9437184]{0:T(1024)(128)(4,1)} %bitcast.14), calls=%async_computation.6 | async-start | bytes 8388608
  40.3 6.5 %slice-start.5 = ((s8[9437184]{0:T(1024)(128)(4,1)}), s8[4194304]{0:T(1024)(128)(4,1)S(1)}, s32[]{:S(2)}) async-start(s8[9437184]{0:T(1024)(128)(4,1)} %bitcast.14), calls=%async_computation.7 | async-start | bytes 8388608
  49.4 50.3 %slice-start = ((s8[9437184]{0:T(1024)(128)(4,1)}), s8[1048576]{0:T(1024)(128)(4,1)S(1)}, s32[]{:S(2)}) async-start(s8[9437184]{0:T(1024)(128)(4,1)} %bitcast.12), calls=%async_computation.2 | async-start | bytes 2097152
  49.5 136.4 %all-reduce.5.cloned.1.call-start = ((), (), s32[]{:S(2)}) async-start(), calls=%async_computation | async-start | bytes 1572864 | tf_op jit(solution)/shard_map/psum | solution.py:32
  93.5 6.3 %slice-start.1 = ((s8[9437184]{0:T(1024)(128)(4,1)}), s8[4194304]{0:T(1024)(128)(4,1)S(1)}, s32[]{:S(2)}) async-start(s8[9437184]{0:T(1024)(128)(4,1)} %bitcast.12), calls=%async_computation.3 | async-start | bytes 8388608
  93.5 6.6 %slice-start.2 = ((s8[9437184]{0:T(1024)(128)(4,1)}), s8[4194304]{0:T(1024)(128)(4,1)S(1)}, s32[]{:S(2)}) async-start(s8[9437184]{0:T(1024)(128)(4,1)} %bitcast.12), calls=%async_computation.4 | async-start | bytes 8388608
  93.5 6.7 %copy-start = (f32[64,3072]{1,0:T(8,128)S(1)}, f32[64,3072]{1,0:T(8,128)}, u32[]{:S(2)}) copy-start(f32[64,3072]{1,0:T(8,128)} %get-tuple-element.5) | copy-start | bytes 2359300
Sparse Core Ops, SparseCore 0:
  49.6 43.8 all-reduce.6
  154.1 31.7 all-reduce.4
where the time goes:
time: 221 us
  blocking collectives  77.6 us (35%)
  waiting for transfers between devices  67.6 us (31%)
  matrix products  42.5 us (19%)
  local copies, waits for them, and re-layouts  19.1 us (9%)
  between operations  14.1 us (6%)
    psum x1, blocking collectives, on_device(): out_tan = lax.psum(partial_value, ('col', 'depth')).astype(jnp.bfloat16)  44.5 us
    psum x1, waiting for transfers between devices, on_device(): hidden, hidden_tan = lax.psum((hidden, hidden_tan), 'row')  44 us
    all_gather x1, blocking collectives, on_device(): gathered = lax.all_gather(tokens, ('col', 'depth'), axis=0, tiled=True)  33.1 us
    psum x1, waiting for transfers between devices, on_device(): backward = lax.psum(backward, 'row')  23.6 us
    unnamed x15, local copies, waits for them, and re-layouts  19.1 us
    dot_general x1, matrix products, on_device(): lax.dot_general(gathered, back_hidden, (((0,), (0,)), ((), ())), preferre...  9.56 us
    dot_general x1, matrix products, on_device(): lax.dot_general(active, out_tan, (((0,), (0,)), ((), ())), preferred_elem...  8.3 us
    dot_general x1, matrix products, on_device(): lax.dot_general(out_tan, second_weight, (((1,), (1,)), ((), ())), preferr...  7.5 us
  transfers between devices with their start and end apart: 2, of which 2 were waited for; matrix products, arithmetic and copies ran while one was open for 4% of the time, Pallas kernels for 0%

commit v1 on v0

--- a/solution.py
+++ b/solution.py
@@ -25,7 +25,7 @@
     partial_value = jnp.dot(
         active_tan, second_weight, preferred_element_type=jnp.float32
     ) + jnp.dot(active, second_tangent, preferred_element_type=jnp.float32)
-    out_tan = lax.psum(partial_value, ("col", "depth")).astype(jnp.bfloat16)
+    out_tan = lax.psum(lax.psum(partial_value, "depth"), "col").astype(jnp.bfloat16)
     backward = lax.dot_general(
         out_tan, second_weight, (((1,), (1,)), ((), ())), preferred_element_type=jnp.float32
     )

time: 221 us -> 232 us (1.050)
  waiting for transfers between devices: 67.6 us -> 107 us
  blocking collectives: 77.6 us -> 48.2 us
    psum x0 -> x1, waiting for transfers between devices: none -> 37.1 us  [on_device(): lax.psum(partial_value, 'depth')]
    psum x1, blocking collectives: 44.5 us -> 15.1 us  [on_device(): lax.psum(lax.psum(partial_value, 'depth'), 'col').astype(jnp.bfloat16)]
    psum x1, waiting for transfers between devices: 23.6 us -> 26.3 us  [on_device(): backward = lax.psum(backward, 'row')]
  transfers between devices with their start and end apart: 2 -> 3, of which waited for: 2 -> 3; matrix products, arithmetic and copies ran while one was open for 4% -> 4% of each run, Pallas kernels for 0% -> 0%
where the time goes in v1:
time: 232 us
  waiting for transfers between devices  107 us (46%)
  blocking collectives  48.2 us (21%)
  matrix products  43.2 us (19%)
  local copies, waits for them, and re-layouts  19.1 us (8%)
  between operations  13.8 us (6%)
    psum x1, waiting for transfers between devices, on_device(): hidden, hidden_tan = lax.psum((hidden, hidden_tan), 'row')  44 us
    psum x1, waiting for transfers between devices, on_device(): lax.psum(partial_value, 'depth')  37.1 us
    all_gather x1, blocking collectives, on_device(): gathered = lax.all_gather(tokens, ('col', 'depth'), axis=0, tiled=True)  33.1 us
    psum x1, waiting for transfers between devices, on_device(): backward = lax.psum(backward, 'row')  26.3 us
    unnamed x15, local copies, waits for them, and re-layouts  19.1 us
    psum x1, blocking collectives, on_device(): lax.psum(lax.psum(partial_value, 'depth'), 'col').astype(jnp.bfloat16)  15.1 us
    dot_general x1, matrix products, on_device(): lax.dot_general(gathered, back_hidden, (((0,), (0,)), ((), ())), preferre...  9.57 us
    dot_general x1, matrix products, on_device(): lax.dot_general(active, out_tan, (((0,), (0,)), ((), ())), preferred_elem...  8.3 us
  transfers between devices with their start and end apart: 3, of which 3 were waited for; matrix products, arithmetic and copies ran while one was open for 4% of the time, Pallas kernels for 0%

profile of v1, /device:TPU:0, one launch (start us, length us, event | category | flops | bytes accessed | tf_op | source)
XLA Modules:
  0.0 231.9 jit_solution(9456652540085575845)
XLA Ops:
  7.2 0.0 slice-start.3
  7.2 0.0 all-reduce.10.cloned.1.call-start
  7.2 33.1 %all_gather.3 = bf16[64,1536]{1,0:T(8,128)(2,1)S(1)} all-gather(bf16[8,1536]{1,0:T(8,128)(2,1)} %param.5), channel_id=1, replica_groups=mesh['row'=4,'col'=2,'depth'=4] {'col','depth'}, dimensions={0}, use_global_device_ids=true | all-gather | bytes 221184 | tf_op jit(solution)/shard_map/all_gather | solution.py:20
  40.3 0.0 slice-start.4
  40.3 0.0 slice-start.5
  40.3 6.5 %fusion.12 = f32[64,3072]{1,0:T(8,128)} fusion(bf16[64,1536]{1,0:T(8,128)(2,1)S(1)} %all_gather.3, bf16[1536,3072]{1,0:T(8,128)(2,1)} %param.7), kind=kOutput, calls=%fused_computation.18 | convolution fusion | flops 603979776 | bytes 10420224 | tf_op jit(solution)/shard_map/dot_general | solution.py:22
  46.8 0.0 slice-done.3
  46.8 0.0 slice-done.4
  46.8 0.0 slice-done.5
  46.8 2.6 %fusion.11 = f32[64,3072]{1,0:T(8,128)} fusion(bf16[64,1536]{1,0:T(8,128)(2,1)S(1)} %all_gather.3, bf16[1536,3072]{1,0:T(8,128)(2,1)S(1)} %bitcast.15), kind=kOutput, calls=%fused_computation.17 | convolution fusion | flops 603979776 | bytes 10420224 | tf_op jit(solution)/shard_map/dot_general | solution.py:21
  49.4 0.0 slice-start
  49.4 0.0 all-reduce.10.cloned.1.call-update
  49.5 0.0 all-reduce.6.cloned.1.call-start
  49.5 44.0 %all-reduce.10.cloned.1.call-done = (f32[64,3072]{1,0:T(8,128)}, f32[64,3072]{1,0:T(8,128)}) async-done(((f32[64,3072]{1,0:T(8,128)}, f32[64,3072]{1,0:T(8,128)}), (f32[64,3072]{1,0:T(8,128)}, f32[64,3072]{1,0:T(8,128)})) %all-reduce.10.cloned.1.call-update) | async-done | bytes 1572880 | tf_op jit(solution)/shard_map/psum | solution.py:23
  93.5 0.0 slice-start.1
  93.5 0.0 slice-start.2
  93.5 6.3 %fusion.5 = f32[64,1536]{1,0:T(8,128)S(1)} fusion(bf16[3072,1536]{1,0:T(8,128)(2,1)} %param.8, f32[64,3072]{1,0:T(8,128)} %get-tuple-element.4, f32[64,3072]{1,0:T(8,128)} %get-tuple-element.5), kind=kOutput, calls=%fused_computation.13 | convolution fusion | flops 607715328 | bytes 11403264 | tf_op jit(solution)/shard_map/dot_general | solution.py:25
  99.8 0.0 slice-done
  99.8 0.0 slice-done.1
  99.8 0.3 slice-done.2
  100.1 0.1 copy-done
  100.2 2.5 %convolution_add_fusion = f32[64,1536]{1,0:T(8,128)} fusion(f32[64,1536]{1,0:T(8,128)S(1)} %fusion.5, bf16[3072,1536]{1,0:T(8,128)(2,1)S(1)} %bitcast.13, f32[64,3072]{1,0:T(8,128)S(1)} %copy-done), kind=kOutput, calls=%fused_computation.2 | convolution fusion | flops 605847552 | bytes 11010048 | tf_op jit(solution)/shard_map/dot_general | solution.py:27
  102.8 0.0 all-reduce.6.cloned.1.call-update
  102.8 0.0 all-reduce.8.cloned.1.call-start
  102.8 37.1 %all-reduce.6.cloned.1.call-done = f32[64,1536]{1,0:T(8,128)} async-done(((f32[64,1536]{1,0:T(8,128)}), f32[64,1536]{1,0:T(8,128)}) %all-reduce.6.cloned.1.call-update) | async-done | bytes 393232 | tf_op jit(solution)/shard_map/psum | solution.py:28
  140.0 15.1 %all-reduce.11 = bf16[64,1536]{1,0:T(8,128)(2,1)S(1)} all-reduce(f32[64,1536]{1,0:T(8,128)} %all-reduce.6.cloned.1.call-done), channel_id=1, replica_groups=mesh['row'=4,'col'=2,'depth'=4] {'col'}, use_global_device_ids=true, to_apply=%region_3.0 | all-reduce | flops 98304 | bytes 589824 | tf_op jit(solution)/shard_map/psum | solution.py:28
  155.0 7.5 %fusion.13 = f32[64,3072]{1,0:T(8,128)} fusion(bf16[64,1536]{1,0:T(8,128)(2,1)S(1)} %all-reduce.11, bf16[3072,1536]{1,0:T(8,128)(2,1)} %param.8), kind=kOutput, calls=%fused_computation.19 | convolution fusion | flops 603979776 | bytes 10420224 | tf_op jit(solution)/shard_map/dot_general | solution.py:29
  162.5 0.0 all-reduce.8.cloned.1.call-update
  162.6 8.3 %convolution_multiply_fusion = f32[3072,1536]{1,0:T(8,128)} fusion(bf16[64,1536]{1,0:T(8,128)(2,1)S(1)} %all-reduce.11, f32[64,3072]{1,0:T(8,128)S(1)} %copy-done), kind=kOutput, calls=%fused_computation.1 | convolution fusion | flops 610467840 | bytes 19857408 | tf_op jit(solution)/shard_map/dot_general | solution.py:36
  170.9 26.3 %all-reduce.8.cloned.1.call-done = f32[64,3072]{1,0:T(8,128)} async-done(((f32[64,3072]{1,0:T(8,128)}), f32[64,3072]{1,0:T(8,128)}) %all-reduce.8.cloned.1.call-update) | async-done | bytes 786448 | tf_op jit(solution)/shard_map/psum | solution.py:32
  197.1 9.6 %multiply_bitcast_fusion = f32[1536,3072]{0,1:T(8,128)} fusion(bf16[64,1536]{1,0:T(8,128)(2,1)S(1)} %all_gather.3, f32[64,3072]{1,0:T(8,128)} %all-reduce.8.cloned.1.call-done, f32[64,3072]{1,0:T(8,128)S(1)} %copy-done), kind=kOutput, calls=%fused_computation | convolution fusion | flops 612433920 | bytes 20643840 | tf_op jit(solution)/shard_map/dot_general | solution.py:42
  206.7 18.6 %copy.7 = f32[1536,3072]{1,0:T(8,128)} copy(f32[1536,3072]{0,1:T(8,128)} %multiply_bitcast_fusion) | data formatting | bytes 37748736
  (3 shorter events, 0.0 us)
Async XLA Ops:
  7.2 39.6 %slice-start.3 = ((s8[9437184]{0:T(1024)(128)(4,1)}), s8[1048576]{0:T(1024)(128)(4,1)S(1)}, s32[]{:S(2)}) async-start(s8[9437184]{0:T(1024)(128)(4,1)} %bitcast.14), calls=%async_computation.6 | async-start | bytes 2097152
  7.2 86.3 %all-reduce.10.cloned.1.call-start = ((), (), s32[]{:S(2)}) async-start(), calls=%async_computation.2 | async-start | bytes 3145728 | tf_op jit(solution)/shard_map/psum | solution.py:23
  40.3 6.5 %slice-start.4 = ((s8[9437184]{0:T(1024)(128)(4,1)}), s8[4194304]{0:T(1024)(128)(4,1)S(1)}, s32[]{:S(2)}) async-start(s8[9437184]{0:T(1024)(128)(4,1)} %bitcast.14), calls=%async_computation.7 | async-start | bytes 8388608
  40.3 6.5 %slice-start.5 = ((s8[9437184]{0:T(1024)(128)(4,1)}), s8[4194304]{0:T(1024)(128)(4,1)S(1)}, s32[]{:S(2)}) async-start(s8[9437184]{0:T(1024)(128)(4,1)} %bitcast.14), calls=%async_computation.8 | async-start | bytes 8388608
  49.4 50.3 %slice-start = ((s8[9437184]{0:T(1024)(128)(4,1)}), s8[1048576]{0:T(1024)(128)(4,1)S(1)}, s32[]{:S(2)}) async-start(s8[9437184]{0:T(1024)(128)(4,1)} %bitcast.12), calls=%async_computation.3 | async-start | bytes 2097152
  49.5 90.5 %all-reduce.6.cloned.1.call-start = ((), (), s32[]{:S(2)}) async-start(), calls=%async_computation | async-start | bytes 786432 | tf_op jit(solution)/shard_map/psum | solution.py:28
  93.5 6.3 %slice-start.1 = ((s8[9437184]{0:T(1024)(128)(4,1)}), s8[4194304]{0:T(1024)(128)(4,1)S(1)}, s32[]{:S(2)}) async-start(s8[9437184]{0:T(1024)(128)(4,1)} %bitcast.12), calls=%async_computation.4 | async-start | bytes 8388608
  93.5 6.6 %slice-start.2 = ((s8[9437184]{0:T(1024)(128)(4,1)}), s8[4194304]{0:T(1024)(128)(4,1)S(1)}, s32[]{:S(2)}) async-start(s8[9437184]{0:T(1024)(128)(4,1)} %bitcast.12), calls=%async_computation.5 | async-start | bytes 8388608
  93.5 6.7 %copy-start = (f32[64,3072]{1,0:T(8,128)S(1)}, f32[64,3072]{1,0:T(8,128)}, u32[]{:S(2)}) copy-start(f32[64,3072]{1,0:T(8,128)} %get-tuple-element.5) | copy-start | bytes 2359300
  102.8 94.3 %all-reduce.8.cloned.1.call-start = ((), (), s32[]{:S(2)}) async-start(), calls=%async_computation.1 | async-start | bytes 1572864 | tf_op jit(solution)/shard_map/psum | solution.py:32
Sparse Core Ops, SparseCore 0:
  49.6 43.8 all-reduce.9
  102.9 37.0 all-reduce.5
  162.7 34.3 all-reduce.7
